TPU v7x, 512 devices: a whole 4x4x16 slice. The times are simulated.
512 devices in a mesh: seq: 16 (over y, x), head: 32 (over z, core).
Axes of the slice: x: 4, y: 4, z: 16, core: 2. Of those that a mesh axis runs over, the one named last changes fastest.
Arguments:
- query: bfloat16 [65536, 8192], P(('seq', 'head')), may hold values from -10 to 10
- sampled_key_value: bfloat16 [2, 65536, 1024], P(None, ('seq', 'head')), may hold values from -6 to 6
- cached_prompt_key_value: bfloat16 [2, 1024, 1024], P(None, 'seq'), may hold values from -6 to 6
- ancestor_block: int32 [512], replicated, may hold values from -1 to 511, as said below
Outputs:
- attended: bfloat16 [65536, 8192], P(('seq', 'head'))
Inputs may be any that keep to these rules, and one draw needn't show every extreme that they name: `ancestor_block`: A block whose entry is not -1 has a parent whose own entry is -1. Groups are aligned runs of 32 blocks; half the blocks of every group have a parent, and for every pair of groups the number of blocks of the one whose parent lies in the other is either 0 or exactly 2.
All inputs are finite; a program needn't handle non-finite values.
Results may differ from a plain program's by a relative error of at most 0.0049.
Values may be sent and summed in bfloat16 or wider, within the bound.
A program may use at most 64 MiB of HBM per device.

v0:
```python
import math

import jax
import jax.numpy as jnp
from jax import lax
from jax.sharding import PartitionSpec as P

QUERY_HEADS = 64
KEY_VALUE_HEADS = 8
HEAD_SIZE = 128
TREE_BLOCK_SIZE = 128
CAP = 2


def body(query, sampled_key_value, cached_prompt_key_value, ancestor_block):
    groups = lax.axis_size("seq")
    total_head_count = lax.axis_size("head")
    group_index = lax.axis_index("seq")
    head_index = lax.axis_index("head")
    token_per_device = query.shape[0]
    per_device = QUERY_HEADS // total_head_count
    query_per_key_ratio = QUERY_HEADS // KEY_VALUE_HEADS
    pair_head = head_index * per_device // query_per_key_ratio
    group_blocks = token_per_device * total_head_count // TREE_BLOCK_SIZE
    group_tokens = group_blocks * TREE_BLOCK_SIZE
    inv_root = 1.0 / math.sqrt(HEAD_SIZE)
    exchanged = lax.all_to_all(
        query.reshape(token_per_device, total_head_count, per_device * HEAD_SIZE),
        "head",
        split_axis=1,
        concat_axis=0,
        tiled=True,
    )
    query_rows = exchanged.reshape(group_blocks, TREE_BLOCK_SIZE, per_device, HEAD_SIZE)
    spread_layout = jnp.repeat(
        sampled_key_value.reshape(2, token_per_device, KEY_VALUE_HEADS, HEAD_SIZE),
        total_head_count // KEY_VALUE_HEADS,
        axis=2,
    )
    local_pair = lax.all_to_all(
        spread_layout, "head", split_axis=2, concat_axis=1, tiled=True
    ).reshape(2, group_blocks, TREE_BLOCK_SIZE, HEAD_SIZE)
    prompt_all = lax.all_gather(cached_prompt_key_value, "seq", axis=1, tiled=True)
    prompt_pair = lax.dynamic_slice_in_dim(prompt_all, pair_head * HEAD_SIZE, HEAD_SIZE, 2)
    prompt_length = prompt_pair.shape[1]
    parents = ancestor_block.reshape(groups, group_blocks)
    has_parent = parents >= 0
    source = jnp.where(has_parent, parents // group_blocks, -1)
    parent_place = jnp.where(has_parent, parents % group_blocks, 0)
    block_iota = jnp.arange(group_blocks, dtype=jnp.int32)
    earlier = block_iota[None, :] < block_iota[:, None]
    same_source = (
        (source[:, :, None] == source[:, None, :]) & has_parent[:, None, :] & earlier[None]
    )
    slot_rank = jnp.sum(same_source.astype(jnp.int32), axis=2)
    slot_iota = jnp.arange(CAP, dtype=jnp.int32)
    from_here = has_parent & (source == group_index)
    slot_hot = ((slot_rank[:, :, None] == slot_iota[None, None, :]) & from_here[:, :, None]).astype(
        jnp.bfloat16
    )
    place_hot = (parent_place[:, :, None] == block_iota[None, None, :]).astype(jnp.bfloat16)
    select = jnp.einsum(
        "djc,djl->dcl", slot_hot, place_hot, preferred_element_type=jnp.float32
    ).astype(jnp.bfloat16)
    outgoing = jnp.einsum(
        "dcl,klbe->dckbe", select, local_pair, preferred_element_type=jnp.float32
    ).astype(jnp.bfloat16)
    incoming = lax.all_to_all(outgoing, "seq", split_axis=0, concat_axis=0, tiled=True)
    own_source = lax.dynamic_index_in_dim(source, group_index, 0, keepdims=False)
    own_rank = lax.dynamic_index_in_dim(slot_rank, group_index, 0, keepdims=False)
    own_parent = lax.dynamic_index_in_dim(has_parent, group_index, 0, keepdims=False)
    flat_slot = own_source * CAP + own_rank
    picker = (
        (flat_slot[:, None] == jnp.arange(groups * CAP, dtype=jnp.int32)[None, :])
        & own_parent[:, None]
    ).astype(jnp.bfloat16)
    parent_pair = jnp.einsum(
        "js,skbe->kjbe",
        picker,
        incoming.reshape(groups * CAP, 2, TREE_BLOCK_SIZE, HEAD_SIZE),
        preferred_element_type=jnp.float32,
    ).astype(jnp.bfloat16)
    tile_blocks = min(group_blocks, max(1, 512 // TREE_BLOCK_SIZE))
    tile_count = group_blocks // tile_blocks
    causal = (
        jnp.arange(TREE_BLOCK_SIZE, dtype=jnp.int32)[:, None]
        >= jnp.arange(TREE_BLOCK_SIZE, dtype=jnp.int32)[None, :]
    )

    def attend(tile_index):
        first_block = tile_index * tile_blocks
        query_block_tile = lax.dynamic_slice_in_dim(query_rows, first_block, tile_blocks, 0)
        self_block_pair = lax.dynamic_slice_in_dim(local_pair, first_block, tile_blocks, 1)
        distant_pair = lax.dynamic_slice_in_dim(parent_pair, first_block, tile_blocks, 1)
        tile_parent = lax.dynamic_slice_in_dim(own_parent, first_block, tile_blocks, 0)
        prompt_scores = jnp.einsum(
            "bqhd,kd->bhqk", query_block_tile, prompt_pair[0], preferred_element_type=jnp.float32
        )
        own_scores = jnp.einsum(
            "tjux,tox->tujo",
            query_block_tile,
            self_block_pair[0],
            preferred_element_type=jnp.float32,
        )
        far_scores = jnp.einsum(
            "tjux,tox->tujo", query_block_tile, distant_pair[0], preferred_element_type=jnp.float32
        )
        scores = jnp.concatenate([prompt_scores, own_scores, far_scores], axis=3) * inv_root
        visible = jnp.concatenate(
            [
                jnp.ones((tile_blocks, 1, TREE_BLOCK_SIZE, prompt_length), bool),
                jnp.broadcast_to(causal, (tile_blocks, 1, TREE_BLOCK_SIZE, TREE_BLOCK_SIZE)),
                jnp.broadcast_to(
                    tile_parent[:, None, None, None],
                    (tile_blocks, 1, TREE_BLOCK_SIZE, TREE_BLOCK_SIZE),
                ),
            ],
            axis=3,
        )
        scores = jnp.where(visible, scores, -jnp.inf)
        row_peak = jnp.max(scores, axis=3, keepdims=True)
        shifted = jnp.exp(scores - row_peak)
        row_total = jnp.sum(shifted, axis=3, keepdims=True)
        weights = (shifted / row_total).astype(jnp.bfloat16)
        result = jnp.einsum(
            "bhqk,kd->bqhd",
            weights[..., :prompt_length],
            prompt_pair[1],
            preferred_element_type=jnp.float32,
        )
        result = result + jnp.einsum(
            "vote,vem->vtom",
            weights[..., prompt_length : prompt_length + TREE_BLOCK_SIZE],
            self_block_pair[1],
            preferred_element_type=jnp.float32,
        )
        result = result + jnp.einsum(
            "vote,vem->vtom",
            weights[..., prompt_length + TREE_BLOCK_SIZE :],
            distant_pair[1],
            preferred_element_type=jnp.float32,
        )
        return result.astype(jnp.bfloat16)

    attended = lax.map(attend, jnp.arange(tile_count, dtype=jnp.int32))
    returned = lax.all_to_all(
        attended.reshape(group_tokens, 1, per_device * HEAD_SIZE),
        "head",
        split_axis=0,
        concat_axis=1,
        tiled=True,
    )
    return returned.reshape(token_per_device, QUERY_HEADS * HEAD_SIZE)


def solution(mesh):
    placed = (P(("seq", "head"), None), P(None, ("seq", "head"), None), P(None, "seq", None), P())
    return jax.shard_map(
        body, mesh=mesh, in_specs=placed, out_specs=P(("seq", "head"), None), check_vma=False
    )
```

profile of v0, /device:TPU:1, one launch (start us, length us, event | category | flops | bytes accessed | tf_op | source)
XLA Modules:
  0.0 531.4 jit_solution(11793505163231997722)
XLA Ops:
  6.5 1.0 copy-done
  7.7 1.8 broadcast_in_dim.25
  9.5 16.9 %all-to-all-start.1 = ((bf16[2,128,32,128]{3,1,0,2:T(8,128)(2,1)}), bf16[2,128,32,128]{3,1,0,2:T(8,128)(2,1)S(1)}, u32[]{:S(2)}, u32[]{:S(2)}) async-start(bf16[2,128,32,128]{3,1,0,2:T(8,128)(2,1)} %bitcast.145), calls=%async_computation.1 | async-start | bytes 4194304 | tf_op jit(solution)/shard_map/all_to_all | solution.py:40
  27.3 97.4 %all-to-all-done.1 = bf16[2,128,32,128]{3,1,0,2:T(8,128)(2,1)S(1)} async-done(((bf16[2,128,32,128]{3,1,0,2:T(8,128)(2,1)}), bf16[2,128,32,128]{3,1,0,2:T(8,128)(2,1)S(1)}, u32[]{:S(2)}, u32[]{:S(2)}) %all-to-all-start.1) | async-done | bytes 2097184 | tf_op jit(solution)/shard_map/all_to_all | solution.py:40
  124.7 1.4 fusion.41
  126.2 1.9 copy.71
  128.0 6.8 %all-to-all-start.2 = ((bf16[16,2,2,128,128]{4,3,2,1,0:T(8,128)(2,1)}), bf16[16,2,2,128,128]{4,3,2,1,0:T(8,128)(2,1)S(1)}, u32[]{:S(2)}, u32[]{:S(2)}) async-start(bf16[16,2,2,128,128]{4,3,2,1,0:T(8,128)(2,1)} %copy.71), calls=%async_computation.2 | async-start | bytes 4194304 | tf_op jit(solution)/shard_map/all_to_all | solution.py:68
  135.5 4.1 copy.67
  139.7 24.8 %all-to-all-done.2 = bf16[16,2,2,128,128]{4,3,2,1,0:T(8,128)(2,1)S(1)} async-done(((bf16[16,2,2,128,128]{4,3,2,1,0:T(8,128)(2,1)}), bf16[16,2,2,128,128]{4,3,2,1,0:T(8,128)(2,1)S(1)}, u32[]{:S(2)}, u32[]{:S(2)}) %all-to-all-start.2) | async-done | bytes 2097184 | tf_op jit(solution)/shard_map/all_to_all | solution.py:68
  164.5 1.4 copy-done.2
  165.8 10.3 %all-to-all-start = ((bf16[128,32,256]{0,2,1:T(8,128)(2,1)}), bf16[128,32,256]{0,2,1:T(8,128)(2,1)S(1)}, u32[]{:S(2)}, u32[]{:S(2)}) async-start(bf16[128,32,256]{0,2,1:T(8,128)(2,1)} %bitcast.146), calls=%async_computation | async-start | bytes 4194304 | tf_op jit(solution)/shard_map/all_to_all | solution.py:27
  176.2 25.1 %all-gather.2.cloned.1.call-done = bf16[2,1024,1024]{2,1,0:T(8,128)(2,1)} async-done(((bf16[2,64,1024]{2,1,0:T(8,128)(2,1)}), bf16[2,1024,1024]{2,1,0:T(8,128)(2,1)}) %all-gather.2.cloned.1.call-update) | async-done | bytes 4194320 | tf_op jit(solution)/shard_map/all_gather | solution.py:43
  201.3 1.1 constant_dynamic-slice_fusion.4
  202.4 4.4 convert_bitcast_fusion
  206.8 68.0 %all-to-all-done = bf16[128,32,256]{0,2,1:T(8,128)(2,1)S(1)} async-done(((bf16[128,32,256]{0,2,1:T(8,128)(2,1)}), bf16[128,32,256]{0,2,1:T(8,128)(2,1)S(1)}, u32[]{:S(2)}, u32[]{:S(2)}) %all-to-all-start) | async-done | bytes 2097184 | tf_op jit(solution)/shard_map/all_to_all | solution.py:27
  274.8 90.3 %while.11 = (s32[]{:T(128)}, bf16[8,4,128,2,128]{4,3,2,1,0:T(2,128)(2,1)}, s32[8]{0:T(128)S(1)}, pred[32]{0:T(512)(128)(4,1)S(1)}, bf16[32,128,2,128]{1,3,2,0:T(...) while((s32[]{:T(128)}, ...), condition=%wide.region_4.5_spmd.clone, body=%wide.region_1.4_spmd.clone.sunk | while | flops 683296000 | bytes 33077500 | solution.py:145
  275.9 1.2 constant_dynamic-slice_fusion.6
  278.2 1.2 convolution_bitcast_fusion.10
  279.8 1.9 exponential_reduce_fusion.2
  281.7 1.3 divide_convert_fusion.2
  283.9 1.1 fusion.83
  287.2 1.2 constant_dynamic-slice_fusion.6
  289.4 1.2 convolution_bitcast_fusion.10
  291.1 1.9 exponential_reduce_fusion.2
  293.0 1.3 divide_convert_fusion.2
  295.2 1.1 fusion.83
  298.5 1.2 constant_dynamic-slice_fusion.6
  300.7 1.2 convolution_bitcast_fusion.10
  302.4 1.9 exponential_reduce_fusion.2
  304.3 1.3 divide_convert_fusion.2
  306.5 1.1 fusion.83
  309.8 1.2 constant_dynamic-slice_fusion.6
  312.0 1.2 convolution_bitcast_fusion.10
  313.7 1.9 exponential_reduce_fusion.2
  315.5 1.3 divide_convert_fusion.2
  317.8 1.1 fusion.83
  321.1 1.2 constant_dynamic-slice_fusion.6
  323.3 1.2 convolution_bitcast_fusion.10
  324.9 1.9 exponential_reduce_fusion.2
  326.8 1.3 divide_convert_fusion.2
  329.1 1.1 fusion.83
  332.3 1.2 constant_dynamic-slice_fusion.6
  334.6 1.2 convolution_bitcast_fusion.10
  336.2 1.9 exponential_reduce_fusion.2
  338.1 1.3 divide_convert_fusion.2
  340.4 1.1 fusion.83
  343.6 1.2 constant_dynamic-slice_fusion.6
  345.9 1.2 convolution_bitcast_fusion.10
  347.5 1.9 exponential_reduce_fusion.2
  349.4 1.3 divide_convert_fusion.2
  351.6 1.1 fusion.83
  354.9 1.2 constant_dynamic-slice_fusion.6
  357.1 1.2 convolution_bitcast_fusion.10
  358.8 1.9 exponential_reduce_fusion.2
  360.7 1.3 divide_convert_fusion.2
  362.9 1.1 fusion.83
  365.1 13.5 %reshape.189 = bf16[4096,1,256]{2,1,0:T(2,128)(2,1)} reshape(bf16[8,4,128,2,128]{4,3,2,1,0:T(2,128)(2,1)} %get-tuple-element.52) | data formatting | bytes 4194304 | tf_op jit(solution)/shard_map/reshape | solution.py:147
  379.1 21.6 %reduce = bf16[4096,256]{1,0:T(8,128)(2,1)S(1)} reduce(bf16[4096,1,256]{2,1,0:T(2,128)(2,1)} %reshape.189, bf16[]{:T(256)} %broadcast.167), dimensions={1}, to_apply=%reshape.189.reduce_sub_computation | reduce | bytes 4194306 | tf_op jit(solution)/shard_map/reshape | solution.py:147
  400.7 2.0 reshape.190
  402.7 105.7 %all_to_all.50 = bf16[32,2,16384]{2,1,0:T(2,128)(2,1)S(1)} all-to-all(bf16[32,2,16384]{2,1,0:T(2,128)(2,1)} %reshape.190), channel_id=1, replica_groups=mesh['seq'=16,'head'=32] {'head'}, dimensions={0} | all-to-all | bytes 4194304 | tf_op jit(solution)/shard_map/all_to_all | solution.py:146
  508.4 6.7 %reshape.191 = bf16[4096,1,256]{2,1,0:T(2,128)(2,1)} reshape(bf16[32,2,16384]{2,1,0:T(2,128)(2,1)S(1)} %all_to_all.50) | data formatting | bytes 4194304
  515.1 2.5 copy.104
  517.7 2.9 copy.78
  520.5 4.1 copy.79
  (124 shorter events, 33.6 us)
Async XLA Ops:
  6.5 1.0 copy-start
  9.5 16.9 %copy-start.3 = (s32[512]{0:T(512)S(1)}, s32[512]{0:T(512)}, u32[]{:S(2)}) copy-start(s32[512]{0:T(512)} %param.9) | copy-start | bytes 6148
  9.5 115.2 %all-to-all-start.1 = ((bf16[2,128,32,128]{3,1,0,2:T(8,128)(2,1)}), bf16[2,128,32,128]{3,1,0,2:T(8,128)(2,1)S(1)}, u32[]{:S(2)}, u32[]{:S(2)}) async-start(bf16[2,128,32,128]{3,1,0,2:T(8,128)(2,1)} %bitcast.145), calls=%async_computation.1 | async-start | bytes 4194304 | tf_op jit(solution)/shard_map/all_to_all | solution.py:40
  124.7 1.4 copy-start.1
  128.0 36.4 %all-to-all-start.2 = ((bf16[16,2,2,128,128]{4,3,2,1,0:T(8,128)(2,1)}), bf16[16,2,2,128,128]{4,3,2,1,0:T(8,128)(2,1)S(1)}, u32[]{:S(2)}, u32[]{:S(2)}) async-start(bf16[16,2,2,128,128]{4,3,2,1,0:T(8,128)(2,1)} %copy.71), calls=%async_computation.2 | async-start | bytes 4194304 | tf_op jit(solution)/shard_map/all_to_all | solution.py:68
  134.8 66.5 %all-gather.2.cloned.1.call-start = ((), (), s32[]{:S(2)}) async-start(), calls=%async_computation.4 | async-start | bytes 4456448 | tf_op jit(solution)/shard_map/all_gather | solution.py:43
  164.5 1.4 copy-start.2
  165.8 109.0 %all-to-all-start = ((bf16[128,32,256]{0,2,1:T(8,128)(2,1)}), bf16[128,32,256]{0,2,1:T(8,128)(2,1)S(1)}, u32[]{:S(2)}, u32[]{:S(2)}) async-start(bf16[128,32,256]{0,2,1:T(8,128)(2,1)} %bitcast.146), calls=%async_computation | async-start | bytes 4194304 | tf_op jit(solution)/shard_map/all_to_all | solution.py:27
Sparse Core Ops, SparseCore 0:
  138.6 62.6 all-gather.1
where the time goes:
time: 533 us; the launch traced here: 531 us
  waiting for transfers between devices  216 us (41%)
  blocking collectives  106 us (20%)
  local copies, waits for them, and re-layouts  67.3 us (13%)
  other arithmetic  49.3 us (9%)
  matrix products  40.3 us (8%)
  starting transfers between devices  34 us (6%)
  between operations  13.5 us (3%)
    all_to_all x1, blocking collectives, body(): lax.all_to_all(attended.reshape(group_tokens, 1, per_device * HEAD_SIZE),...  106 us
    all_to_all x1, waiting for transfers between devices, body(): lax.all_to_all(spread_layout, 'head', split_axis=2, concat_axis=1, tiled=...  97.4 us
    all_to_all x1, waiting for transfers between devices, body(): lax.all_to_all(query.reshape(token_per_device, total_head_count, per_devi...  68 us
    all_gather x1, waiting for transfers between devices, body(): lax.all_gather(cached_prompt_key_value, 'seq', axis=1, tiled=True)  25.1 us
    all_to_all x1, waiting for transfers between devices, body(): lax.all_to_all(outgoing, 'seq', split_axis=0, concat_axis=0, tiled=True)  24.8 us
    reshape x1, other arithmetic, body(): attended.reshape(group_tokens, 1, per_device * HEAD_SIZE)  21.6 us
    unnamed x12, local copies, waits for them, and re-layouts  17.8 us
    all_to_all x1, starting transfers between devices, body(): lax.all_to_all(spread_layout, 'head', split_axis=2, concat_axis=1, tiled=...  16.9 us
  transfers between devices with their start and end apart: 4, of which 4 were waited for; matrix products, arithmetic and copies ran while one was open for 2% of the time, Pallas kernels for 0%

commit v1 on v0

v1 whole, which is shorter than its diff:
```python
import functools
import math

import jax
import jax.numpy as jnp
from jax import lax
from jax.experimental import pallas as pl
from jax.experimental.pallas import tpu as pltpu
from jax.sharding import PartitionSpec as P

QUERY_HEADS = 64
KEY_VALUE_HEADS = 8
HEAD_SIZE = 128
BLOCK = 128
RATIO = QUERY_HEADS // KEY_VALUE_HEADS
CAP = 2
PIECE = 8
EXP2_SCALE = math.log2(math.e) / math.sqrt(HEAD_SIZE)


def dot(left, right, contract_right):
    return lax.dot_general(
        left, right, (((1,), (contract_right,)), ((), ())), preferred_element_type=jnp.float32
    )


def attention_kernel(parent_ref, q_ref, own_ref, prompt_ref, far_ref, o_ref, k_s, v_s, *, heads):
    prompt = prompt_ref.shape[1]
    total = prompt + 2 * BLOCK
    for target, source in ((k_s, 0), (v_s, 1)):
        target[0:prompt, 0:HEAD_SIZE] = prompt_ref[source]
        target[prompt : prompt + BLOCK, 0:HEAD_SIZE] = own_ref[source]
        target[prompt + BLOCK : total, 0:HEAD_SIZE] = far_ref[source]
    v_s[:, HEAD_SIZE:] = jnp.ones((total, HEAD_SIZE), jnp.bfloat16)
    has_parent = parent_ref[0] >= 0
    rows = heads * BLOCK
    row = lax.broadcasted_iota(jnp.int32, (rows, BLOCK), 0) % BLOCK
    col = lax.broadcasted_iota(jnp.int32, (rows, BLOCK), 1)
    causal = col <= row
    for step in range(RATIO // heads):
        spans = [
            slice((step * heads + i) * HEAD_SIZE, (step * heads + i + 1) * HEAD_SIZE)
            for i in range(heads)
        ]
        q = jnp.concatenate([q_ref[:, span] for span in spans], axis=0)
        scores = dot(q, k_s[...], 1)
        own = jnp.where(causal, scores[:, prompt : prompt + BLOCK], -jnp.inf)
        far = jnp.where(has_parent, scores[:, prompt + BLOCK :], -jnp.inf)
        scores = jnp.concatenate([scores[:, :prompt], own, far], axis=1)
        peak = jnp.max(scores, axis=1, keepdims=True)
        weights = jnp.exp2(scores * EXP2_SCALE - peak * EXP2_SCALE)
        summed = dot(weights.astype(jnp.bfloat16), v_s[...], 0)
        out = (summed[:, :HEAD_SIZE] / summed[:, HEAD_SIZE:]).astype(jnp.bfloat16)
        for i, span in enumerate(spans):
            o_ref[:, span] = out[i * BLOCK : (i + 1) * BLOCK]


def attention(parent, query, own, prompt, far):
    prompt_tokens = prompt.shape[1]
    total = prompt_tokens + 2 * BLOCK
    group = RATIO * HEAD_SIZE
    return pl.pallas_call(
        functools.partial(attention_kernel, heads=2),
        grid_spec=pltpu.PrefetchScalarGridSpec(
            num_scalar_prefetch=1,
            grid=(KEY_VALUE_HEADS,),
            in_specs=[
                pl.BlockSpec((BLOCK, group), lambda j, p: (0, j)),
                pl.BlockSpec((2, BLOCK, HEAD_SIZE), lambda j, p: (0, 0, j)),
                pl.BlockSpec((2, prompt_tokens, HEAD_SIZE), lambda j, p: (0, 0, j)),
                pl.BlockSpec((2, BLOCK, HEAD_SIZE), lambda j, p: (0, 0, j)),
            ],
            out_specs=pl.BlockSpec((BLOCK, group), lambda j, p: (0, j)),
            scratch_shapes=[
                pltpu.VMEM((total, HEAD_SIZE), jnp.bfloat16),
                pltpu.VMEM((total, 2 * HEAD_SIZE), jnp.bfloat16),
            ],
        ),
        out_shape=jax.ShapeDtypeStruct((BLOCK, QUERY_HEADS * HEAD_SIZE), jnp.bfloat16),
        compiler_params=pltpu.CompilerParams(vmem_limit_bytes=40 * 2**20),
        name="attention",
    )(parent, query, own, prompt, far)


def pick_kernel(index_ref, x_ref, o_ref):
    def step(i, carry):
        o_ref[i] = x_ref[index_ref[i]]
        return carry

    lax.fori_loop(0, o_ref.shape[0], step, 0)


def pick(index, x):
    return pl.pallas_call(
        pick_kernel,
        in_specs=[
            pl.BlockSpec(memory_space=pltpu.SMEM),
            pl.BlockSpec(memory_space=pltpu.VMEM),
        ],
        out_specs=pl.BlockSpec(memory_space=pltpu.VMEM),
        out_shape=jax.ShapeDtypeStruct((index.shape[0],) + x.shape[1:], x.dtype),
        name="pick",
    )(index, x)


def tables(ancestor_block, groups, blocks, group_index):
    parents = ancestor_block.reshape(groups, blocks)
    has_parent = parents >= 0
    source = jnp.where(has_parent, parents // blocks, -1)
    place = jnp.where(has_parent, parents % blocks, 0)
    iota = jnp.arange(blocks, dtype=jnp.int32)
    earlier = iota[None, :] < iota[:, None]
    same = (source[:, :, None] == source[:, None, :]) & has_parent[:, None, :] & earlier[None]
    rank = jnp.sum(same.astype(jnp.int32), axis=2)
    mine = source == group_index
    slots = jnp.arange(CAP, dtype=jnp.int32)
    hot = mine[:, None, :] & (rank[:, None, :] == slots[None, :, None])
    outgoing = jnp.sum(jnp.where(hot, place[:, None, :], 0), axis=2).reshape(groups * CAP)
    own_source = lax.dynamic_index_in_dim(source, group_index, 0, keepdims=False)
    own_rank = lax.dynamic_index_in_dim(rank, group_index, 0, keepdims=False)
    incoming = jnp.where(own_source >= 0, own_source * CAP + own_rank, 0)
    return outgoing, incoming


def body(query, sampled_key_value, cached_prompt_key_value, ancestor_block):
    groups = lax.axis_size("seq")
    blocks = lax.axis_size("head")
    group_index = lax.axis_index("seq")
    head_index = lax.axis_index("head")
    width = KEY_VALUE_HEADS * HEAD_SIZE
    outgoing, incoming = tables(ancestor_block, groups, blocks, group_index)
    parent = lax.dynamic_slice_in_dim(ancestor_block, group_index * blocks + head_index, 1, 0)
    prompt = lax.all_gather(cached_prompt_key_value, "seq", axis=1, tiled=True)
    pieces = sampled_key_value.reshape(blocks, PIECE, width)
    held = lax.all_to_all(pieces, "head", split_axis=0, concat_axis=0, tiled=True)
    sent = pick(outgoing, held)
    landed = lax.all_to_all(sent, "seq", split_axis=0, concat_axis=0, tiled=True)
    spread = pick(incoming, landed)
    far = lax.all_to_all(spread, "head", split_axis=0, concat_axis=0, tiled=True)
    far = far.reshape(2, BLOCK, width)
    return attention(parent, query, sampled_key_value, prompt, far)


def solution(mesh):
    placed = (P(("seq", "head"), None), P(None, ("seq", "head"), None), P(None, "seq", None), P())
    return jax.shard_map(
        body, mesh=mesh, in_specs=placed, out_specs=P(("seq", "head"), None), check_vma=False
    )
```

time: 533 us -> 156 us (0.29)
  waiting for transfers between devices: 216 us -> 81.1 us
  blocking collectives: 106 us -> 0 us
  local copies, waits for them, and re-layouts: 67.3 us -> 6.44 us
  other arithmetic: 49.3 us -> 1.11 us
  matrix products: 40.3 us -> 0 us
  Pallas kernels: 0 us -> 24.8 us
    all_to_all x3, waiting for transfers between devices: 190 us -> 80.4 us  [the longest x1 32.3 us: body(): lax.all_to_all(spread, 'head', split_axis=0, concat_axis=0, tiled=True)]
    all_to_all x1 -> x0, blocking collectives: 106 us -> none  [body(): lax.all_to_all(attended.reshape(group_tokens, 1, per_device * HEAD_SIZE),...]
    dot_general x51 -> x0, matrix products: 40.3 us -> none  [the longest x8 9.53 us: attend(): jnp.einsum('tjux,tox->tujo', query_block_tile, self_block_pair[0], prefer...]
    all_gather x1, waiting for transfers between devices: 25.1 us -> 0.01 us  [body(): prompt = lax.all_gather(cached_prompt_key_value, 'seq', axis=1, tiled=True)]
    pallas_call x0 -> x3, Pallas kernels: none -> 24.8 us  [the longest x1 20.7 us: attention(): pl.pallas_call(functools.partial(attention_kernel, heads=2), grid_spec=pl...]
    reshape x1 -> x0, other arithmetic: 21.6 us -> none  [body(): attended.reshape(group_tokens, 1, per_device * HEAD_SIZE)]
    reshape x5 -> x2, local copies, waits for them, and re-layouts: 18.3 us -> 1.34 us  [the longest x1 0.76 us: tables(): parents = ancestor_block.reshape(groups, blocks)]
    sub x8 -> x0, other arithmetic: 15 us -> none  [attend(): shifted = jnp.exp(scores - row_peak)]
  transfers between devices with their start and end apart: 4 -> 4, of which waited for: 4 -> 3; matrix products, arithmetic and copies ran while one was open for 2% -> 2% of each run, Pallas kernels for 0% -> 3%
where the time goes in v1:
time: 156 us
  waiting for transfers between devices  81.1 us (52%)
  starting transfers between devices  28.9 us (19%)
  Pallas kernels  24.8 us (16%)
  between operations  13.5 us (9%)
  local copies, waits for them, and re-layouts  6.44 us (4%)
    all_to_all x1, waiting for transfers between devices, body(): lax.all_to_all(spread, 'head', split_axis=0, concat_axis=0, tiled=True)  32.3 us
    all_to_all x1, waiting for transfers between devices, body(): lax.all_to_all(pieces, 'head', split_axis=0, concat_axis=0, tiled=True)  31.5 us
    pallas_call x1, Pallas kernels, attention(): pl.pallas_call(functools.partial(attention_kernel, heads=2), grid_spec=pl...  20.7 us
    all_to_all x1, starting transfers between devices, body(): lax.all_to_all(pieces, 'head', split_axis=0, concat_axis=0, tiled=True)  16.8 us
    all_to_all x1, waiting for transfers between devices, body(): lax.all_to_all(sent, 'seq', split_axis=0, concat_axis=0, tiled=True)  16.6 us
    all_to_all x1, starting transfers between devices, body(): lax.all_to_all(sent, 'seq', split_axis=0, concat_axis=0, tiled=True)  6.75 us
    all_to_all x1, starting transfers between devices, body(): lax.all_to_all(spread, 'head', split_axis=0, concat_axis=0, tiled=True)  5.35 us
    pallas_call x2, Pallas kernels, pick(): pl.pallas_call(pick_kernel, in_specs=[pl.BlockSpec(memory_space=pltpu.SME...  4.12 us
  transfers between devices with their start and end apart: 4, of which 3 were waited for; matrix products, arithmetic and copies ran while one was open for 2% of the time, Pallas kernels for 3%

profile of v1, /device:TPU:1, one launch (start us, length us, event | category | flops | bytes accessed | tf_op | source)
XLA Modules:
  0.0 155.7 jit_solution(11752643411389426030)
XLA Ops:
  6.5 0.0 all-gather.2.cloned.1.call-start
  6.5 0.7 all-gather.2.cloned.1.call-update
  7.3 16.8 %all-to-all-start = ((bf16[32,8,1024]{2,1,0:T(8,128)(2,1)}), bf16[32,8,1024]{2,1,0:T(8,128)(2,1)S(1)}, u32[]{:S(2)}, u32[]{:S(2)}) async-start(bf16[32,8,1024]{2,1,0:T(8,128)(2,1)} %bitcast.4), calls=%async_computation | async-start | bytes 1048576 | tf_op jit(solution)/shard_map/all_to_all | solution.py:135
  24.0 0.8 reshape.137
  24.8 0.5 convert_reduce_fusion
  25.3 0.1 select_reduce_fusion
  25.4 0.1 copy.5
  25.5 0.6 reshape.138.index_ref
  26.1 0.0 copy-start.1
  26.1 0.0 copy-start.2
  26.1 31.5 %all-to-all-done.x_ref = bf16[32,8,1024]{2,1,0:T(8,128)(2,1)S(1)} async-done(((bf16[32,8,1024]{2,1,0:T(8,128)(2,1)}), bf16[32,8,1024]{2,1,0:T(8,128)(2,1)S(1)}, u32[]{:S(2)}, u32[]{:S(2)}) %all-to-all-start) | async-done | bytes 524320 | tf_op jit(solution)/shard_map/all_to_all | solution.py:135
  57.5 0.0 copy-start.3
  57.5 0.8 copy-done.3
  58.3 2.1 %pick.2 = bf16[32,8,1024]{2,1,0:T(8,128)(2,1)} custom-call(s32[32]{0:T(128)} %reshape.138.index_ref, bf16[32,8,1024]{2,1,0:T(8,128)(2,1)} %copy-done.3), custom_call_target="tpu_custom_call" | custom-call | tf_op jit(solution)/shard_map/pick/pallas_call | solution.py:94
  60.4 6.8 %all-to-all-start.1 = ((bf16[32,8,1024]{2,1,0:T(8,128)(2,1)}), bf16[32,8,1024]{2,1,0:T(8,128)(2,1)S(1)}, u32[]{:S(2)}, u32[]{:S(2)}) async-start(bf16[32,8,1024]{2,1,0:T(8,128)(2,1)} %pick.2), calls=%async_computation.1 | async-start | bytes 1048576 | tf_op jit(solution)/shard_map/all_to_all | solution.py:137
  67.2 0.5 fusion.5.index_ref
  67.6 16.6 %all-to-all-done.1.x_ref = bf16[32,8,1024]{2,1,0:T(8,128)(2,1)S(1)} async-done(((bf16[32,8,1024]{2,1,0:T(8,128)(2,1)}), bf16[32,8,1024]{2,1,0:T(8,128)(2,1)S(1)}, u32[]{:S(2)}, u32[]{:S(2)}) %all-to-all-start.1) | async-done | bytes 524320 | tf_op jit(solution)/shard_map/all_to_all | solution.py:137
  84.3 0.0 copy-start.4
  84.3 0.8 copy-done.4
  85.1 2.1 %pick.3 = bf16[32,8,1024]{2,1,0:T(8,128)(2,1)} custom-call(s32[32]{0:T(128)} %fusion.5.index_ref, bf16[32,8,1024]{2,1,0:T(8,128)(2,1)} %copy-done.4), custom_call_target="tpu_custom_call" | custom-call | tf_op jit(solution)/shard_map/pick/pallas_call | solution.py:94
  87.1 5.3 %all-to-all-start.2 = ((bf16[32,8,1024]{2,1,0:T(8,128)(2,1)}), bf16[32,8,1024]{2,1,0:T(8,128)(2,1)S(1)}, u32[]{:S(2)}, u32[]{:S(2)}) async-start(bf16[32,8,1024]{2,1,0:T(8,128)(2,1)} %pick.3), calls=%async_computation.2 | async-start | bytes 1048576 | tf_op jit(solution)/shard_map/all_to_all | solution.py:139
  92.5 1.2 dynamic_slice.10.parent_ref
  93.7 32.3 %all-to-all-done.2 = bf16[32,8,1024]{2,1,0:T(8,128)(2,1)S(1)} async-done(((bf16[32,8,1024]{2,1,0:T(8,128)(2,1)}), bf16[32,8,1024]{2,1,0:T(8,128)(2,1)S(1)}, u32[]{:S(2)}, u32[]{:S(2)}) %all-to-all-start.2) | async-done | bytes 524320 | tf_op jit(solution)/shard_map/all_to_all | solution.py:139
  126.0 0.0 all-gather.2.cloned.1.call-done.prompt_ref
  126.0 0.0 copy-done.1
  126.0 0.0 copy-done.2
  126.0 0.0 copy-start
  126.0 2.2 %copy-done = bf16[2,1024,1024]{2,1,0:T(8,128)(2,1)S(1)} copy-done((bf16[2,1024,1024]{2,1,0:T(8,128)(2,1)S(1)}, bf16[2,1024,1024]{2,1,0:T(8,128)(2,1)}, u32[]{:S(2)}) %copy-start) | copy-done | bytes 4194328
  128.2 20.7 %attention.1 = bf16[128,8192]{1,0:T(8,128)(2,1)} custom-call(s32[1]{0:T(128)} %dynamic_slice.10.parent_ref, bf16[128,8192]{1,0:T(8,128)(2,1)S(1)} %copy-done.1, bf16[2,128,1024]{2,1,0:T(8,128)(2,1)S(1)} %copy-done.2, bf16[2,1024,1024]{2,1,0:T(8,128)(2,1)S(1)} %copy-done, bf16[2,128,1024]{2,1,0:T(8,128)(2,1)S(1)} %bitcast.5), custom_call_target="tpu_custom_call" | custom-call | tf_op jit(solution)/shard_map/attention/pallas_call | solution.py:62
  (3 shorter events, 0.0 us)
Async XLA Ops:
  6.5 119.5 %all-gather.2.cloned.1.call-start = ((), (), s32[]{:S(2)}) async-start(), calls=%async_computation.3 | async-start | bytes 4456448 | tf_op jit(solution)/shard_map/all_gather | solution.py:133
  7.3 50.3 %all-to-all-start = ((bf16[32,8,1024]{2,1,0:T(8,128)(2,1)}), bf16[32,8,1024]{2,1,0:T(8,128)(2,1)S(1)}, u32[]{:S(2)}, u32[]{:S(2)}) async-start(bf16[32,8,1024]{2,1,0:T(8,128)(2,1)} %bitcast.4), calls=%async_computation | async-start | bytes 1048576 | tf_op jit(solution)/shard_map/all_to_all | solution.py:135
  26.1 99.9 %copy-start.1 = (bf16[128,8192]{1,0:T(8,128)(2,1)S(1)}, bf16[128,8192]{1,0:T(8,128)(2,1)}, u32[]{:S(2)}) copy-start(bf16[128,8192]{1,0:T(8,128)(2,1)} %q_ref.1) | copy-start | bytes 6291460
  26.1 99.9 %copy-start.2 = (bf16[2,128,1024]{2,1,0:T(8,128)(2,1)S(1)}, bf16[2,128,1024]{2,1,0:T(8,128)(2,1)}, u32[]{:S(2)}) copy-start(bf16[2,128,1024]{2,1,0:T(8,128)(2,1)} %own_ref.1) | copy-start | bytes 1572868
  57.5 0.8 copy-start.3
  60.4 23.9 %all-to-all-start.1 = ((bf16[32,8,1024]{2,1,0:T(8,128)(2,1)}), bf16[32,8,1024]{2,1,0:T(8,128)(2,1)S(1)}, u32[]{:S(2)}, u32[]{:S(2)}) async-start(bf16[32,8,1024]{2,1,0:T(8,128)(2,1)} %pick.2), calls=%async_computation.1 | async-start | bytes 1048576 | tf_op jit(solution)/shard_map/all_to_all | solution.py:137
  84.3 0.8 copy-start.4
  87.1 38.9 %all-to-all-start.2 = ((bf16[32,8,1024]{2,1,0:T(8,128)(2,1)}), bf16[32,8,1024]{2,1,0:T(8,128)(2,1)S(1)}, u32[]{:S(2)}, u32[]{:S(2)}) async-start(bf16[32,8,1024]{2,1,0:T(8,128)(2,1)} %pick.3), calls=%async_computation.2 | async-start | bytes 1048576 | tf_op jit(solution)/shard_map/all_to_all | solution.py:139
  126.0 2.2 %copy-start = (bf16[2,1024,1024]{2,1,0:T(8,128)(2,1)S(1)}, bf16[2,1024,1024]{2,1,0:T(8,128)(2,1)}, u32[]{:S(2)}) copy-start(bf16[2,1024,1024]{2,1,0:T(8,128)(2,1)} %all-gather.2.cloned.1.call-done.prompt_ref) | copy-start | bytes 12582916
Sparse Core Ops, SparseCore 0:
  10.3 77.3 all-gather.1

commit v2 on v1

v2 whole, which is shorter than its diff:
```python
import functools
import math

import jax
import jax.numpy as jnp
from jax import lax
from jax.experimental import pallas as pl
from jax.experimental.pallas import tpu as pltpu
from jax.sharding import PartitionSpec as P

QUERY_HEADS = 64
KEY_VALUE_HEADS = 8
HEAD_SIZE = 128
BLOCK = 128
RATIO = QUERY_HEADS // KEY_VALUE_HEADS
CAP = 2
WIDTH = KEY_VALUE_HEADS * HEAD_SIZE
PIECE_ROWS = 16
PIECE_COLS = WIDTH // 2
CHUNKS = 2
CHUNK_COLS = PIECE_COLS // CHUNKS
HALF = WIDTH // 2
HEADS = 2
EXP2_SCALE = math.log2(math.e) / math.sqrt(HEAD_SIZE)
MESH = pl.DeviceIdType.MESH


def dot(left, right, contract_right):
    return lax.dot_general(
        left, right, (((1,), (contract_right,)), ((), ())), preferred_element_type=jnp.float32
    )


def piece_of(ref, index, chunk):
    row = pl.multiple_of(((index // 2) % (BLOCK // PIECE_ROWS)) * PIECE_ROWS, PIECE_ROWS)
    col = pl.multiple_of((index % 2) * PIECE_COLS + chunk * CHUNK_COLS, CHUNK_COLS)
    kv = index // (2 * (BLOCK // PIECE_ROWS))
    return ref.at[kv, pl.ds(row, PIECE_ROWS), pl.ds(col, CHUNK_COLS)]


def kernel(
    groups,
    blocks,
    anc_ref,
    q_ref,
    own_ref,
    shard_ref,
    o_ref,
    prompt_0,
    prompt_1,
    held_0,
    held_1,
    sent_0,
    sent_1,
    landed_0,
    landed_1,
    spread_0,
    spread_1,
    far_0,
    far_1,
    k_s,
    v_s,
    acc_s,
    peak_s,
    out_tab,
    in_tab,
    held_send,
    held_recv,
    land_send,
    land_recv,
    far_send,
    far_recv,
    prompt_send,
    prompt_recv,
    pass_send,
    pass_recv,
    local_sem,
):
    held, sent = (held_0, held_1), (sent_0, sent_1)
    landed, spread = (landed_0, landed_1), (spread_0, spread_1)
    prompt, far = (prompt_0, prompt_1), (far_0, far_1)
    group = lax.axis_index("seq")
    place = lax.axis_index("head")
    core = place % 2
    twin = place + 1 - 2 * core
    shard_rows = shard_ref.shape[1]
    prompt_rows = groups * shard_rows

    barrier = pltpu.get_barrier_semaphore()

    def greet(axis, size, me):
        def step(k, carry):
            pl.semaphore_signal(
                barrier, inc=1, device_id={axis: (me + k) % size}, device_id_type=MESH
            )
            return carry

        lax.fori_loop(1, size, step, 0)

    greet("head", blocks, place)
    greet("seq", groups, group)

    own_pieces = [
        pltpu.make_async_copy(piece_of(own_ref, place, c), held[c].at[0], local_sem.at[c])
        for c in range(CHUNKS)
    ]
    own_rows = pl.ds(pl.multiple_of(group * shard_rows, shard_rows), shard_rows)
    own_shards = [
        pltpu.make_async_copy(
            shard_ref.at[kv, :, pl.ds(half * HALF, HALF)],
            prompt[half].at[kv, own_rows],
            local_sem.at[6 + 2 * half + kv],
        )
        for kv in range(2)
        for half in range(2)
    ]
    for copy in own_pieces + own_shards:
        copy.start()

    def outgoing(k, carry):
        base = ((group + k) % groups) * blocks

        def look(j, found):
            count, first, second = found
            parent = anc_ref[base + j]
            hit = (parent >> 5) == group
            slot = (parent - place) & (blocks - 1)
            first = jnp.where(hit & (count == 0), slot, first)
            second = jnp.where(hit & (count == 1), slot, second)
            return count + hit.astype(jnp.int32), first, second

        zero = jnp.int32(0)
        _, first, second = lax.fori_loop(0, blocks, look, (zero, zero, zero), unroll=8)
        out_tab[k * CAP] = first
        out_tab[k * CAP + 1] = second
        return carry

    lax.fori_loop(0, groups, outgoing, 0)

    def incoming(k, carry):
        j = (place + k) % blocks
        parent = anc_ref[group * blocks + j]
        source = parent >> 5

        def look(i, rank):
            same = ((anc_ref[group * blocks + i] >> 5) == source) & (i < j)
            return jnp.where(same, 1, rank)

        rank = lax.fori_loop(0, blocks, look, jnp.int32(0), unroll=8)
        slot = ((source - group) & (groups - 1)) * CAP + rank
        in_tab[k] = jnp.where(parent >= 0, slot, 0)
        return carry

    lax.fori_loop(0, blocks, incoming, 0)

    pl.semaphore_wait(barrier, blocks + groups - 2)

    def send_held(c):
        def step(k, carry):
            peer = (place + k) % blocks
            pltpu.make_async_remote_copy(
                src_ref=piece_of(own_ref, peer, c),
                dst_ref=held[c].at[blocks - k],
                send_sem=held_send.at[c],
                recv_sem=held_recv.at[c, blocks - k],
                device_id={"head": peer},
                device_id_type=MESH,
            ).start()
            return carry

        lax.fori_loop(1, blocks, step, 0)

    def shard_cols(half):
        return pl.ds(half * HALF, HALF)

    def send_shard(half):
        def step(k, carry):
            peer = (group + k) % groups
            pltpu.make_async_remote_copy(
                src_ref=shard_ref.at[core, :, shard_cols(half)],
                dst_ref=prompt[half].at[core, own_rows],
                send_sem=prompt_send.at[half],
                recv_sem=prompt_recv.at[half, groups - k],
                device_id={"seq": peer},
                device_id_type=MESH,
            ).start()
            return carry

        lax.fori_loop(1, groups, step, 0)

    def pass_shard(half):
        def step(k, carry):
            source = (group + k) % groups
            rows = pl.ds(pl.multiple_of(source * shard_rows, shard_rows), shard_rows)
            view = prompt[half].at[core, rows]
            pltpu.make_async_copy(view, view, prompt_recv.at[half, k]).wait()
            pltpu.make_async_remote_copy(
                src_ref=view,
                dst_ref=view,
                send_sem=pass_send.at[half],
                recv_sem=pass_recv.at[half, k],
                device_id={"head": twin},
                device_id_type=MESH,
            ).start()
            return carry

        lax.fori_loop(1, groups, step, 0)

    def wait_bytes(view, sem):
        pltpu.make_async_copy(view, view, sem).wait()

    def others(kv, half):
        return prompt[half].at[kv, pl.ds(0, prompt_rows - shard_rows)]

    def relay_groups(c):
        def arrive(k, carry):
            wait_bytes(held[c].at[k], held_recv.at[c, k])
            return carry

        lax.fori_loop(1, blocks, arrive, 0)
        own_pieces[c].wait()

        def pick(i, carry):
            sent[c][i] = held[c][out_tab[i]]
            return carry

        lax.fori_loop(0, groups * CAP, pick, 0)
        here = pltpu.make_async_copy(
            sent[c].at[pl.ds(0, CAP)], landed[c].at[pl.ds(0, CAP)], local_sem.at[4 + c]
        )
        here.start()

        def step(k, carry):
            pltpu.make_async_remote_copy(
                src_ref=sent[c].at[pl.ds(k * CAP, CAP)],
                dst_ref=landed[c].at[pl.ds((groups - k) * CAP, CAP)],
                send_sem=land_send.at[c],
                recv_sem=land_recv.at[c, groups - k],
                device_id={"seq": (group + k) % groups},
                device_id_type=MESH,
            ).start()
            return carry

        lax.fori_loop(1, groups, step, 0)
        here.wait()

    def relay_blocks(c):
        def arrive(k, carry):
            wait_bytes(landed[c].at[pl.ds(k * CAP, CAP)], land_recv.at[c, k])
            return carry

        lax.fori_loop(1, groups, arrive, 0)

        def pick(i, carry):
            spread[c][i] = landed[c][in_tab[i]]
            return carry

        lax.fori_loop(0, blocks, pick, 0)
        here = pltpu.make_async_copy(spread[c].at[0], far[c].at[place], local_sem.at[2 + c])
        here.start()

        def step(k, carry):
            pltpu.make_async_remote_copy(
                src_ref=spread[c].at[k],
                dst_ref=far[c].at[place],
                send_sem=far_send.at[c],
                recv_sem=far_recv.at[c, blocks - k],
                device_id={"head": (place + k) % blocks},
                device_id_type=MESH,
            ).start()
            return carry

        lax.fori_loop(1, blocks, step, 0)
        here.wait()

    near = prompt_rows + BLOCK
    rows = HEADS * BLOCK
    row = lax.broadcasted_iota(jnp.int32, (rows, BLOCK), 0) % BLOCK
    col = lax.broadcasted_iota(jnp.int32, (rows, BLOCK), 1)
    causal = col <= row
    v_s[:, HEAD_SIZE:] = jnp.ones((near, HEAD_SIZE), jnp.bfloat16)
    ones = jnp.ones((BLOCK, HEAD_SIZE), jnp.bfloat16)
    has_parent = anc_ref[group * blocks + place] >= 0

    def spans(head, step):
        return [
            pl.ds(
                pl.multiple_of(head * (RATIO * HEAD_SIZE), HEAD_SIZE)
                + (step * HEADS + i) * HEAD_SIZE,
                HEAD_SIZE,
            )
            for i in range(HEADS)
        ]

    def head_cols(head):
        return pl.ds(pl.multiple_of(head * HEAD_SIZE, HEAD_SIZE), HEAD_SIZE)

    def attend_near(half, place_in_half):
        head = half * (KEY_VALUE_HEADS // 2) + place_in_half
        for target, kv in ((k_s, 0), (v_s, 1)):
            target[0:prompt_rows, 0:HEAD_SIZE] = prompt[half][kv, :, head_cols(place_in_half)]
            target[prompt_rows:near, 0:HEAD_SIZE] = own_ref[kv, :, head_cols(head)]
        for step in range(RATIO // HEADS):
            q = jnp.concatenate([q_ref[:, span] for span in spans(head, step)], axis=0)
            scores = dot(q, k_s[...], 1)
            own = jnp.where(causal, scores[:, prompt_rows:], -jnp.inf)
            scores = jnp.concatenate([scores[:, :prompt_rows], own], axis=1)
            peak = jnp.max(scores, axis=1, keepdims=True)
            weights = jnp.exp2(scores * EXP2_SCALE - peak * EXP2_SCALE)
            acc_s[head, step * rows : (step + 1) * rows] = dot(
                weights.astype(jnp.bfloat16), v_s[...], 0
            )
            peak_s[head, step * rows : (step + 1) * rows] = jnp.broadcast_to(
                peak, (rows, HEAD_SIZE)
            )

    def attend_far(c, side, place_in_chunk):
        head = side * (KEY_VALUE_HEADS // 2) + c * 2 + place_in_chunk
        bands = BLOCK // PIECE_ROWS

        def load(kv):
            return jnp.concatenate(
                [
                    far[c][(kv * bands + band) * 2 + side, :, head_cols(place_in_chunk)]
                    for band in range(bands)
                ],
                axis=0,
            )

        keys = load(0)
        values = jnp.concatenate([load(1), ones], axis=1)
        for step in range(RATIO // HEADS):
            here = spans(head, step)
            q = jnp.concatenate([q_ref[:, span] for span in here], axis=0)
            scores = jnp.where(has_parent, dot(q, keys, 1), -jnp.inf)
            before = peak_s[head, step * rows : (step + 1) * rows]
            peak = jnp.maximum(jnp.max(scores, axis=1, keepdims=True), before)
            weights = jnp.exp2((scores - peak) * EXP2_SCALE)
            scale = jnp.exp2((before - peak) * EXP2_SCALE)
            far_sum = dot(weights.astype(jnp.bfloat16), values, 0)
            near_sum = acc_s[head, step * rows : (step + 1) * rows]
            total = near_sum[:, :HEAD_SIZE] * scale + far_sum[:, :HEAD_SIZE]
            norm = near_sum[:, HEAD_SIZE:] * scale + far_sum[:, HEAD_SIZE:]
            out = (total / norm).astype(jnp.bfloat16)
            for i, span in enumerate(here):
                o_ref[:, span] = out[i * BLOCK : (i + 1) * BLOCK]

    def attend(half, first, last):
        def step(i, carry):
            attend_near(half, i)
            return carry

        lax.fori_loop(first, last, step, 0)

    def wait_half(half):
        pass_shard(half)

        def step(k, carry):
            source = (group + k) % groups
            rows = pl.ds(pl.multiple_of(source * shard_rows, shard_rows), shard_rows)
            wait_bytes(prompt[half].at[1 - core, rows], pass_recv.at[half, k])
            return carry

        lax.fori_loop(1, groups, step, 0)

    send_held(0)
    send_shard(0)
    send_held(1)
    send_shard(1)
    for copy in own_shards:
        copy.wait()

    wait_half(0)
    attend(0, 0, 1)
    relay_groups(0)
    attend(0, 1, 3)
    relay_blocks(0)
    attend(0, 3, 4)
    relay_groups(1)
    wait_half(1)
    attend(1, 0, 3)
    relay_blocks(1)
    attend(1, 3, 4)

    for c in range(CHUNKS):
        view = held[c].at[pl.ds(1, blocks - 1)]

        def arrive(k, carry):
            wait_bytes(far[c].at[(place + k) % blocks], far_recv.at[c, k])
            return carry

        lax.fori_loop(1, blocks, arrive, 0)

        def step(i, carry):
            attend_far(c, i // 2, i % 2)
            return carry

        lax.fori_loop(0, KEY_VALUE_HEADS // CHUNKS, step, 0)
        wait_bytes(view, held_send.at[c])
        wait_bytes(sent[c].at[pl.ds(CAP, (groups - 1) * CAP)], land_send.at[c])
        wait_bytes(view, far_send.at[c])
    for half in range(2):
        wait_bytes(others(core, half), prompt_send.at[half])
        wait_bytes(others(core, half), pass_send.at[half])


def body(query, sampled_key_value, cached_prompt_key_value, ancestor_block):
    groups = lax.axis_size("seq")
    blocks = lax.axis_size("head")
    prompt_rows = groups * cached_prompt_key_value.shape[1]
    near = prompt_rows + BLOCK
    bf16 = jnp.bfloat16
    vmem = pl.BlockSpec(memory_space=pltpu.VMEM)
    dma = pltpu.SemaphoreType.DMA
    return pl.pallas_call(
        functools.partial(kernel, groups, blocks),
        in_specs=[pl.BlockSpec(memory_space=pltpu.SMEM), vmem, vmem, vmem],
        out_specs=vmem,
        out_shape=jax.ShapeDtypeStruct(query.shape, query.dtype),
        scratch_shapes=[
            *[pltpu.VMEM((2, prompt_rows, HALF), bf16)] * 2,
            *[pltpu.VMEM((blocks, PIECE_ROWS, CHUNK_COLS), bf16)] * CHUNKS,
            *[pltpu.VMEM((groups * CAP, PIECE_ROWS, CHUNK_COLS), bf16)] * (2 * CHUNKS),
            *[pltpu.VMEM((blocks, PIECE_ROWS, CHUNK_COLS), bf16)] * CHUNKS,
            *[pltpu.VMEM((blocks, PIECE_ROWS, CHUNK_COLS), bf16)] * CHUNKS,
            pltpu.VMEM((near, HEAD_SIZE), bf16),
            pltpu.VMEM((near, 2 * HEAD_SIZE), bf16),
            pltpu.VMEM((KEY_VALUE_HEADS, RATIO * BLOCK, 2 * HEAD_SIZE), jnp.float32),
            pltpu.VMEM((KEY_VALUE_HEADS, RATIO * BLOCK, HEAD_SIZE), jnp.float32),
            pltpu.SMEM((groups * CAP,), jnp.int32),
            pltpu.SMEM((blocks,), jnp.int32),
            dma((CHUNKS,)),
            dma((CHUNKS, blocks)),
            dma((CHUNKS,)),
            dma((CHUNKS, groups)),
            dma((CHUNKS,)),
            dma((CHUNKS, blocks)),
            dma((2,)),
            dma((2, groups)),
            dma((2,)),
            dma((2, groups)),
            dma((10,)),
        ],
        compiler_params=pltpu.CompilerParams(
            collective_id=0, has_side_effects=True, vmem_limit_bytes=60 * 2**20
        ),
        name="tree_attention",
    )(ancestor_block, query, sampled_key_value, cached_prompt_key_value)


def solution(mesh):
    placed = (P(("seq", "head"), None), P(None, ("seq", "head"), None), P(None, "seq", None), P())
    return jax.shard_map(
        body, mesh=mesh, in_specs=placed, out_specs=P(("seq", "head"), None), check_vma=False
    )
```

time: 156 us -> 90.3 us (0.58)
  waiting for transfers between devices: 81.1 us -> 0 us
  Pallas kernels: 24.8 us -> 87 us
  starting transfers between devices: 28.9 us -> 0 us
  between operations: 13.5 us -> 0.01 us
  local copies, waits for them, and re-layouts: 6.44 us -> 3.1 us
    all_to_all x3 -> x0, waiting for transfers between devices: 80.4 us -> none  [the longest x1 32.3 us: body(): lax.all_to_all(spread, 'head', split_axis=0, concat_axis=0, tiled=True)]
    pallas_call x3 -> x1, Pallas kernels: 24.8 us -> 87 us  [body(): pl.pallas_call(functools.partial(kernel, groups, blocks), in_specs=[pl.Bl...]
    all_to_all x3 -> x0, starting transfers between devices: 28.9 us -> none  [the longest x1 16.8 us: body(): lax.all_to_all(pieces, 'head', split_axis=0, concat_axis=0, tiled=True)]
    unnamed x10 -> x1, local copies, waits for them, and re-layouts: 3.78 us -> 3.1 us
  transfers between devices with their start and end apart: 4 -> 0, of which waited for: 3 -> 0; matrix products, arithmetic and copies ran while one was open for 2% -> 0% of each run, Pallas kernels for 3% -> 0%
where the time goes in v2:
time: 90.3 us; the launch traced here: 90.1 us
  Pallas kernels  87 us (96%)
  local copies, waits for them, and re-layouts  3.1 us (3%)
    pallas_call x1, Pallas kernels, body(): pl.pallas_call(functools.partial(kernel, groups, blocks), in_specs=[pl.Bl...  87 us
    unnamed x1, local copies, waits for them, and re-layouts  3.1 us

profile of v2, /device:TPU:1, one launch (start us, length us, event | category | flops | bytes accessed | tf_op | source)
XLA Modules:
  0.0 90.1 jit_solution(13355505580010268512)
XLA Ops:
  0.0 87.0 %tree_attention.1 = bf16[128,8192]{1,0:T(8,128)(2,1)} custom-call(s32[512]{0:T(512)} %anc_ref.1, bf16[128,8192]{1,0:T(8,128)(2,1)} %q_ref.1, bf16[2,128,1024]{2,1,0:T(8,128)(2,1)} %own_ref.1, bf16[2,64,1024]{2,1,0:T(8,128)(2,1)} %shard_ref.1), custom_call_target="tpu_custom_call" | custom-call | tf_op jit(solution)/shard_map/tree_attention/pallas_call | solution.py:415
  87.0 3.1 %copy.6 = bf16[128,8192]{1,0:T(8,128)(2,1)} copy(bf16[128,8192]{1,0:T(8,128)(2,1)} %tree_attention.1) | data formatting | bytes 4194304

commit v3 on v2

--- a/solution.py
+++ b/solution.py
@@ -19,7 +19,9 @@
 PIECE_COLS = WIDTH // 2
 CHUNKS = 2
 CHUNK_COLS = PIECE_COLS // CHUNKS
-HALF = WIDTH // 2
+PARTS = 4
+PART_HEADS = KEY_VALUE_HEADS // PARTS
+PART_COLS = WIDTH // PARTS
 HEADS = 2
 EXP2_SCALE = math.log2(math.e) / math.sqrt(HEAD_SIZE)
 MESH = pl.DeviceIdType.MESH
@@ -48,6 +50,8 @@
     o_ref,
     prompt_0,
     prompt_1,
+    prompt_2,
+    prompt_3,
     held_0,
     held_1,
     sent_0,
@@ -78,7 +82,7 @@
 ):
     held, sent = (held_0, held_1), (sent_0, sent_1)
     landed, spread = (landed_0, landed_1), (spread_0, spread_1)
-    prompt, far = (prompt_0, prompt_1), (far_0, far_1)
+    prompt, far = (prompt_0, prompt_1, prompt_2, prompt_3), (far_0, far_1)
     group = lax.axis_index("seq")
     place = lax.axis_index("head")
     core = place % 2
@@ -107,56 +111,29 @@
     own_rows = pl.ds(pl.multiple_of(group * shard_rows, shard_rows), shard_rows)
     own_shards = [
         pltpu.make_async_copy(
-            shard_ref.at[kv, :, pl.ds(half * HALF, HALF)],
-            prompt[half].at[kv, own_rows],
-            local_sem.at[6 + 2 * half + kv],
+            shard_ref.at[kv, :, pl.ds(part * PART_COLS, PART_COLS)],
+            prompt[part].at[kv, own_rows],
+            local_sem.at[6 + 2 * part + kv],
         )
         for kv in range(2)
-        for half in range(2)
+        for part in range(PARTS)
     ]
     for copy in own_pieces + own_shards:
         copy.start()
 
-    def outgoing(k, carry):
-        base = ((group + k) % groups) * blocks
-
-        def look(j, found):
-            count, first, second = found
-            parent = anc_ref[base + j]
-            hit = (parent >> 5) == group
-            slot = (parent - place) & (blocks - 1)
-            first = jnp.where(hit & (count == 0), slot, first)
-            second = jnp.where(hit & (count == 1), slot, second)
-            return count + hit.astype(jnp.int32), first, second
-
-        zero = jnp.int32(0)
-        _, first, second = lax.fori_loop(0, blocks, look, (zero, zero, zero), unroll=8)
-        out_tab[k * CAP] = first
-        out_tab[k * CAP + 1] = second
-        return carry
-
-    lax.fori_loop(0, groups, outgoing, 0)
-
-    def incoming(k, carry):
-        j = (place + k) % blocks
-        parent = anc_ref[group * blocks + j]
-        source = parent >> 5
-
-        def look(i, rank):
-            same = ((anc_ref[group * blocks + i] >> 5) == source) & (i < j)
-            return jnp.where(same, 1, rank)
-
-        rank = lax.fori_loop(0, blocks, look, jnp.int32(0), unroll=8)
-        slot = ((source - group) & (groups - 1)) * CAP + rank
-        in_tab[k] = jnp.where(parent >= 0, slot, 0)
-        return carry
-
-    lax.fori_loop(0, blocks, incoming, 0)
-
     pl.semaphore_wait(barrier, blocks + groups - 2)
 
+    def farthest_first(send):
+        def step(i, carry):
+            send(blocks // 2 - i)
+            send(blocks // 2 + 1 + i)
+            return carry
+
+        lax.fori_loop(0, blocks // 2 - 1, step, 0)
+        send(1)
+
     def send_held(c):
-        def step(k, carry):
+        def send(k):
             peer = (place + k) % blocks
             pltpu.make_async_remote_copy(
                 src_ref=piece_of(own_ref, peer, c),
@@ -166,21 +143,20 @@
                 device_id={"head": peer},
                 device_id_type=MESH,
             ).start()
-            return carry
-
-        lax.fori_loop(1, blocks, step, 0)
-
-    def shard_cols(half):
-        return pl.ds(half * HALF, HALF)
-
-    def send_shard(half):
+
+        farthest_first(send)
+
+    def shard_cols(part):
+        return pl.ds(part * PART_COLS, PART_COLS)
+
+    def send_shard(part):
         def step(k, carry):
             peer = (group + k) % groups
             pltpu.make_async_remote_copy(
-                src_ref=shard_ref.at[core, :, shard_cols(half)],
-                dst_ref=prompt[half].at[core, own_rows],
-                send_sem=prompt_send.at[half],
-                recv_sem=prompt_recv.at[half, groups - k],
+                src_ref=shard_ref.at[core, :, shard_cols(part)],
+                dst_ref=prompt[part].at[core, own_rows],
+                send_sem=prompt_send.at[part],
+                recv_sem=prompt_recv.at[part, groups - k],
                 device_id={"seq": peer},
                 device_id_type=MESH,
             ).start()
@@ -188,17 +164,17 @@
 
         lax.fori_loop(1, groups, step, 0)
 
-    def pass_shard(half):
+    def pass_shard(part):
         def step(k, carry):
             source = (group + k) % groups
             rows = pl.ds(pl.multiple_of(source * shard_rows, shard_rows), shard_rows)
-            view = prompt[half].at[core, rows]
-            pltpu.make_async_copy(view, view, prompt_recv.at[half, k]).wait()
+            view = prompt[part].at[core, rows]
+            pltpu.make_async_copy(view, view, prompt_recv.at[part, k]).wait()
             pltpu.make_async_remote_copy(
                 src_ref=view,
                 dst_ref=view,
-                send_sem=pass_send.at[half],
-                recv_sem=pass_recv.at[half, k],
+                send_sem=pass_send.at[part],
+                recv_sem=pass_recv.at[part, k],
                 device_id={"head": twin},
                 device_id_type=MESH,
             ).start()
@@ -209,8 +185,8 @@
     def wait_bytes(view, sem):
         pltpu.make_async_copy(view, view, sem).wait()
 
-    def others(kv, half):
-        return prompt[half].at[kv, pl.ds(0, prompt_rows - shard_rows)]
+    def others(kv, part):
+        return prompt[part].at[kv, pl.ds(0, prompt_rows - shard_rows)]
 
     def relay_groups(c):
         def arrive(k, carry):
@@ -259,7 +235,7 @@
         here = pltpu.make_async_copy(spread[c].at[0], far[c].at[place], local_sem.at[2 + c])
         here.start()
 
-        def step(k, carry):
+        def send(k):
             pltpu.make_async_remote_copy(
                 src_ref=spread[c].at[k],
                 dst_ref=far[c].at[place],
@@ -268,9 +244,8 @@
                 device_id={"head": (place + k) % blocks},
                 device_id_type=MESH,
             ).start()
-            return carry
-
-        lax.fori_loop(1, blocks, step, 0)
+
+        farthest_first(send)
         here.wait()
 
     near = prompt_rows + BLOCK
@@ -295,10 +270,10 @@
     def head_cols(head):
         return pl.ds(pl.multiple_of(head * HEAD_SIZE, HEAD_SIZE), HEAD_SIZE)
 
-    def attend_near(half, place_in_half):
-        head = half * (KEY_VALUE_HEADS // 2) + place_in_half
+    def attend_near(part, place_in_part):
+        head = part * PART_HEADS + place_in_part
         for target, kv in ((k_s, 0), (v_s, 1)):
-            target[0:prompt_rows, 0:HEAD_SIZE] = prompt[half][kv, :, head_cols(place_in_half)]
+            target[0:prompt_rows, 0:HEAD_SIZE] = prompt[part][kv, :, head_cols(place_in_part)]
             target[prompt_rows:near, 0:HEAD_SIZE] = own_ref[kv, :, head_cols(head)]
         for step in range(RATIO // HEADS):
             q = jnp.concatenate([q_ref[:, span] for span in spans(head, step)], axis=0)
@@ -345,20 +320,20 @@
             for i, span in enumerate(here):
                 o_ref[:, span] = out[i * BLOCK : (i + 1) * BLOCK]
 
-    def attend(half, first, last):
+    def attend(part):
         def step(i, carry):
-            attend_near(half, i)
-            return carry
-
-        lax.fori_loop(first, last, step, 0)
-
-    def wait_half(half):
-        pass_shard(half)
+            attend_near(part, i)
+            return carry
+
+        lax.fori_loop(0, PART_HEADS, step, 0)
+
+    def wait_part(part):
+        pass_shard(part)
 
         def step(k, carry):
             source = (group + k) % groups
             rows = pl.ds(pl.multiple_of(source * shard_rows, shard_rows), shard_rows)
-            wait_bytes(prompt[half].at[1 - core, rows], pass_recv.at[half, k])
+            wait_bytes(prompt[part].at[1 - core, rows], pass_recv.at[part, k])
             return carry
 
         lax.fori_loop(1, groups, step, 0)
@@ -367,20 +342,60 @@
     send_shard(0)
     send_held(1)
     send_shard(1)
+
+    def outgoing(k, carry):
+        base = ((group + k) % groups) * blocks
+
+        def look(j, found):
+            count, first, second = found
+            parent = anc_ref[base + j]
+            hit = (parent >> 5) == group
+            slot = (parent - place) & (blocks - 1)
+            first = jnp.where(hit & (count == 0), slot, first)
+            second = jnp.where(hit & (count == 1), slot, second)
+            return count + hit.astype(jnp.int32), first, second
+
+        zero = jnp.int32(0)
+        _, first, second = lax.fori_loop(0, blocks, look, (zero, zero, zero), unroll=8)
+        out_tab[k * CAP] = first
+        out_tab[k * CAP + 1] = second
+        return carry
+
+    lax.fori_loop(0, groups, outgoing, 0)
+
+    def incoming(k, carry):
+        j = (place + k) % blocks
+        parent = anc_ref[group * blocks + j]
+        source = parent >> 5
+
+        def look(i, rank):
+            same = ((anc_ref[group * blocks + i] >> 5) == source) & (i < j)
+            return jnp.where(same, 1, rank)
+
+        rank = lax.fori_loop(0, blocks, look, jnp.int32(0), unroll=8)
+        slot = ((source - group) & (groups - 1)) * CAP + rank
+        in_tab[k] = jnp.where(parent >= 0, slot, 0)
+        return carry
+
+    lax.fori_loop(0, blocks, incoming, 0)
+
     for copy in own_shards:
         copy.wait()
 
-    wait_half(0)
-    attend(0, 0, 1)
+    wait_part(0)
+    attend(0)
     relay_groups(0)
-    attend(0, 1, 3)
+    send_shard(2)
+    wait_part(1)
+    attend(1)
     relay_blocks(0)
-    attend(0, 3, 4)
     relay_groups(1)
-    wait_half(1)
-    attend(1, 0, 3)
+    send_shard(3)
+    wait_part(2)
+    attend(2)
     relay_blocks(1)
-    attend(1, 3, 4)
+    wait_part(3)
+    attend(3)
 
     for c in range(CHUNKS):
         view = held[c].at[pl.ds(1, blocks - 1)]
@@ -399,9 +414,9 @@
         wait_bytes(view, held_send.at[c])
         wait_bytes(sent[c].at[pl.ds(CAP, (groups - 1) * CAP)], land_send.at[c])
         wait_bytes(view, far_send.at[c])
-    for half in range(2):
-        wait_bytes(others(core, half), prompt_send.at[half])
-        wait_bytes(others(core, half), pass_send.at[half])
+    for part in range(PARTS):
+        wait_bytes(others(core, part), prompt_send.at[part])
+        wait_bytes(others(core, part), pass_send.at[part])
 
 
 def body(query, sampled_key_value, cached_prompt_key_value, ancestor_block):
@@ -418,7 +433,7 @@
         out_specs=vmem,
         out_shape=jax.ShapeDtypeStruct(query.shape, query.dtype),
         scratch_shapes=[
-            *[pltpu.VMEM((2, prompt_rows, HALF), bf16)] * 2,
+            *[pltpu.VMEM((2, prompt_rows, PART_COLS), bf16)] * PARTS,
             *[pltpu.VMEM((blocks, PIECE_ROWS, CHUNK_COLS), bf16)] * CHUNKS,
             *[pltpu.VMEM((groups * CAP, PIECE_ROWS, CHUNK_COLS), bf16)] * (2 * CHUNKS),
             *[pltpu.VMEM((blocks, PIECE_ROWS, CHUNK_COLS), bf16)] * CHUNKS,
@@ -435,14 +450,14 @@
             dma((CHUNKS, groups)),
             dma((CHUNKS,)),
             dma((CHUNKS, blocks)),
-            dma((2,)),
-            dma((2, groups)),
-            dma((2,)),
-            dma((2, groups)),
-            dma((10,)),
+            dma((PARTS,)),
+            dma((PARTS, groups)),
+            dma((PARTS,)),
+            dma((PARTS, groups)),
+            dma((6 + 2 * PARTS,)),
         ],
         compiler_params=pltpu.CompilerParams(
-            collective_id=0, has_side_effects=True, vmem_limit_bytes=60 * 2**20
+            collective_id=0, has_side_effects=True, vmem_limit_bytes=30 * 2**20
         ),
         name="tree_attention",
     )(ancestor_block, query, sampled_key_value, cached_prompt_key_value)

time: 90.3 us -> 79.1 us (0.88)
  Pallas kernels: 87 us -> 73.2 us
  local copies, waits for them, and re-layouts: 3.1 us -> 5.58 us
    pallas_call x1, Pallas kernels: 87 us -> 73.2 us  [body(): pl.pallas_call(functools.partial(kernel, groups, blocks), in_specs=[pl.Bl...]
    unnamed x1 -> x9, local copies, waits for them, and re-layouts: 3.1 us -> 5.58 us
where the time goes in v3:
time: 79.1 us; the launch traced here: 78.8 us
  Pallas kernels  73.2 us (93%)
  local copies, waits for them, and re-layouts  5.58 us (7%)
    pallas_call x1, Pallas kernels, body(): pl.pallas_call(functools.partial(kernel, groups, blocks), in_specs=[pl.Bl...  73.2 us
    unnamed x9, local copies, waits for them, and re-layouts  5.58 us

profile of v3, /device:TPU:1, one launch (start us, length us, event | category | flops | bytes accessed | tf_op | source)
XLA Modules:
  0.0 78.8 jit_solution(4670734524691635043)
XLA Ops:
  0.0 0.0 copy-start
  0.0 1.6 %copy-done = bf16[128,8192]{1,0:T(8,128)(2,1)S(1)} copy-done((bf16[128,8192]{1,0:T(8,128)(2,1)S(1)}, bf16[128,8192]{1,0:T(8,128)(2,1)}, u32[]{:S(2)}) %copy-start) | copy-done | bytes 2097176
  1.6 0.0 copy-start.1
  1.6 1.0 %copy-done.1 = bf16[2,128,1024]{2,1,0:T(8,128)(2,1)S(1)} copy-done((bf16[2,128,1024]{2,1,0:T(8,128)(2,1)S(1)}, bf16[2,128,1024]{2,1,0:T(8,128)(2,1)}, u32[]{:S(2)}) %copy-start.1) | copy-done | bytes 524312
  2.6 0.0 copy-start.2
  2.6 0.9 %copy-done.2 = bf16[2,64,1024]{2,1,0:T(8,128)(2,1)S(1)} copy-done((bf16[2,64,1024]{2,1,0:T(8,128)(2,1)S(1)}, bf16[2,64,1024]{2,1,0:T(8,128)(2,1)}, u32[]{:S(2)}) %copy-start.2) | copy-done | bytes 262168
  3.6 0.0 copy-start.3
  3.6 0.7 copy-done.3
  4.3 73.2 %tree_attention.1 = bf16[128,8192]{1,0:T(8,128)(2,1)S(1)} custom-call(s32[512]{0:T(512)S(1)} %copy-done.3, bf16[128,8192]{1,0:T(8,128)(2,1)S(1)} %copy-done, bf16[2,128,1024]{2,1,0:T(8,128)(2,1)S(1)} %copy-done.1, bf16[2,64,1024]{2,1,0:T(8,128)(2,1)S(1)} %copy-done.2), custom_call_target="tpu_custom_call" | custom-call | tf_op jit(solution)/shard_map/tree_attention/pallas_call | solution.py:430
  77.5 1.3 %copy.6 = bf16[128,8192]{1,0:T(8,128)(2,1)} copy(bf16[128,8192]{1,0:T(8,128)(2,1)S(1)} %tree_attention.1) | data formatting | bytes 4194304
Async XLA Ops:
  0.0 1.6 %copy-start = (bf16[128,8192]{1,0:T(8,128)(2,1)S(1)}, bf16[128,8192]{1,0:T(8,128)(2,1)}, u32[]{:S(2)}) copy-start(bf16[128,8192]{1,0:T(8,128)(2,1)} %q_ref.1) | copy-start | bytes 6291460
  1.6 1.0 %copy-start.1 = (bf16[2,128,1024]{2,1,0:T(8,128)(2,1)S(1)}, bf16[2,128,1024]{2,1,0:T(8,128)(2,1)}, u32[]{:S(2)}) copy-start(bf16[2,128,1024]{2,1,0:T(8,128)(2,1)} %own_ref.1) | copy-start | bytes 1572868
  2.6 0.9 %copy-start.2 = (bf16[2,64,1024]{2,1,0:T(8,128)(2,1)S(1)}, bf16[2,64,1024]{2,1,0:T(8,128)(2,1)}, u32[]{:S(2)}) copy-start(bf16[2,64,1024]{2,1,0:T(8,128)(2,1)} %shard_ref.1) | copy-start | bytes 786436
  3.6 0.7 copy-start.3
